TPU v7x, 32 devices: a whole 2x2x4 slice. The times are simulated.
32 devices in a mesh: heads: 2 (over x), ctx: 16 (over z, y, core).
Axes of the slice: x: 2, y: 2, z: 4, core: 2. Of those that a mesh axis runs over, the one named last changes fastest.
Arguments:
- queries: bfloat16 [4096, 4096], P('ctx', 'heads'), may hold values from -80 to 80
- keys: bfloat16 [4096, 1024], P('ctx', 'heads'), may hold values from -4.5 to 4.5
- values: bfloat16 [4096, 1024], P('ctx', 'heads'), may hold values from -6 to 6
- doc_ids: int32 [4096], P('ctx'), may hold values from 0 to 3, never falling along the last dimension, each value on 1 to 2048 neighbouring positions
- out_weight: bfloat16 [4096, 4096], P('heads', 'ctx'), may hold values from -0.09375 to 0.09375
Outputs:
- mixed: bfloat16 [4096, 4096], P('ctx', 'heads')
Inputs may be any that keep to these rules, and one draw needn't show every extreme that they name: `doc_ids`: document ids never fall along the tokens; each document has at most 2048 tokens.
All inputs are finite; a program needn't handle non-finite values.
Results may differ from a plain program's by a relative error of at most 0.015.
Values may be sent and summed in bfloat16 or wider, within the bound.
A program may use at most 64 MiB of HBM per device.

v0:
```python
import jax
import jax.numpy as jnp
from jax import lax
from jax.sharding import PartitionSpec as P

HEAD_SIZE = 128
LOOKBACK_WINDOW = 4096
QPG = 4


def passed_along(block, axis, distance):
    devices = range(lax.axis_size(axis))
    route = [(i - distance, i) for i in devices if i - distance in devices]
    return lax.ppermute(block, axis, route)


def body(queries, keys, values, doc_ids, out_weight):
    tok_rows = queries.shape[0]
    groups = keys.shape[1] // HEAD_SIZE
    scale = HEAD_SIZE ** (-0.5)
    q_local = queries.reshape(tok_rows, groups, QPG, HEAD_SIZE)
    here = lax.axis_index("ctx")
    qpos = here * tok_rows + jnp.arange(tok_rows, dtype=jnp.int32)
    reach = LOOKBACK_WINDOW // tok_rows

    def work(state, kblk, vblk, sblk, kstart):
        rowmax, total, accum = state
        scores = (
            jnp.einsum(
                "tgnh,sgh->tgns",
                q_local,
                kblk.reshape(tok_rows, groups, HEAD_SIZE),
                preferred_element_type=jnp.float32,
            )
            * scale
        )
        kpos = kstart + jnp.arange(tok_rows, dtype=jnp.int32)
        vis = (
            (kpos[None, :] <= qpos[:, None])
            & (qpos[:, None] - kpos[None, :] < LOOKBACK_WINDOW)
            & (kpos[None, :] >= 0)
            & (doc_ids[:, None] == sblk[None, :])
        )
        vis = vis[:, None, None, :]
        scores = jnp.where(vis, scores, jnp.float32(-1e30))
        newmax = jnp.maximum(rowmax, jnp.max(scores, axis=-1))
        weights = jnp.where(vis, jnp.exp(scores - newmax[..., None]), jnp.float32(0.0))
        factor = jnp.exp(rowmax - newmax)
        total = total * factor + jnp.sum(weights, axis=-1)
        rounded = weights.astype(jnp.bfloat16)
        contrib = jnp.einsum(
            "tgns,sgh->tgnh",
            rounded,
            vblk.reshape(tok_rows, groups, HEAD_SIZE),
            preferred_element_type=jnp.float32,
        )
        accum = accum * factor[..., None] + contrib
        return (newmax, total, accum)

    def attend(state, kblk, vblk, sblk, kstart):
        return work(state, kblk, vblk, sblk, kstart)

    state = (
        jnp.full((tok_rows, groups, QPG), -1e30, jnp.float32),
        jnp.zeros((tok_rows, groups, QPG), jnp.float32),
        jnp.zeros((tok_rows, groups, QPG, HEAD_SIZE), jnp.float32),
    )
    state = attend(state, keys, values, doc_ids, here * tok_rows)

    def chain_step(depth, carry):
        st, kblk, vblk, sblk = carry
        kblk, vblk, sblk = passed_along((kblk, vblk, sblk), "ctx", 1)
        st = attend(st, kblk, vblk, sblk, (here - depth) * tok_rows)
        return (st, kblk, vblk, sblk)

    state = lax.fori_loop(1, reach + 1, chain_step, (state, keys, values, doc_ids))[0]
    rowmax, total, accum = state
    attn = (
        (accum / total[..., None]).astype(jnp.bfloat16).reshape(tok_rows, groups * QPG * HEAD_SIZE)
    )
    partial_sums = jnp.dot(
        attn,
        lax.all_gather(out_weight, "ctx", axis=1, tiled=True),
        preferred_element_type=jnp.float32,
    )
    return lax.psum_scatter(
        partial_sums.astype(jnp.bfloat16), "heads", scatter_dimension=1, tiled=True
    )


def solution(mesh):
    in_specs = (
        P("ctx", "heads"),
        P("ctx", "heads"),
        P("ctx", "heads"),
        P("ctx"),
        P("heads", "ctx"),
    )
    out_specs = P("ctx", "heads")
    return jax.shard_map(body, mesh=mesh, in_specs=in_specs, out_specs=out_specs, check_vma=False)
```

profile of v0, /device:TPU:24, one launch (start us, length us, event | category | flops | bytes accessed | tf_op | source)
XLA Modules:
  0.0 396.3 jit_solution(7539750365400468989)
XLA Ops:
  17.8 5.7 %bitcast_add_fusion.1 = f32[256,4,4,128]{3,0,2,1:T(8,128)} fusion(f32[4,256,256,4]{2,1,3,0:T(8,128)} %copy-done, f32[256,4,4]{0,2,1:T(4,128)S(1)} %broadcast_maximum_fusion, pred[256,256]{0,1:T(8,128)(4,1)S(1)} %fusion.37, f32[256,4,4]{0,2,1:T(4,128)S(1)} %get-tuple-element.256, bf16[256,4,128,1]{2,1,0,3:T(4,128)(2,1)S(1)} %bitcast.98), kind=kOutput, calls=%fused_computation.32 | convolution fusion | flops 274202624 | bytes 6651904 | tf_op jit(solution)/shard_map/tgns,sgh->tgnh/dot_general | solution.py:51
  23.5 320.2 %while.24 = (s32[]{:T(128)}, f32[256,4,4]{0,2,1:T(4,128)S(1)}, f32[256,4,4]{0,2,1:T(4,128)S(1)}, f32[256,4,4,128]{3,0,2,1:T(8,128)}, bf16[256,512]{0,1:T(8,128)(...) while((s32[]{:T(128)}, f32[256,4,4]{0,2,1:T(4,128)S(1)}, ...), condition=%wide.region_5.6_spmd.clone, body=%wide.region_2.5_spmd.clone.sunk | while | flops 552018944 | bytes 38810448 | solution.py:76
  25.4 3.5 collective-permute-start.1
  31.1 7.6 %collective-permute-done.1 = bf16[256,512]{0,1:T(8,128)(2,1)S(1)} collective-permute-done((bf16[256,512]{0,1:T(8,128)(2,1)S(1)}, bf16[256,512]{0,1:T(8,128)(2,1)S(1)}, u32[]{:S(2)}, u32[]{:S(2)}) %collective-permute-start.1) | collective-permute-done | bytes 262176 | tf_op jit(solution)/shard_map/while/body/eval_jaxpr/ppermute | solution.py:14
  40.7 11.5 %collective-permute-done.2 = bf16[256,512]{0,1:T(8,128)(2,1)S(1)} collective-permute-done((bf16[256,512]{0,1:T(8,128)(2,1)S(1)}, bf16[256,512]{0,1:T(8,128)(2,1)S(1)}, u32[]{:S(2)}, u32[]{:S(2)}) %collective-permute-start.2) | collective-permute-done | bytes 262176 | tf_op jit(solution)/shard_map/while/body/eval_jaxpr/ppermute | solution.py:14
  52.2 1.9 bitcast_add_fusion.3
  61.6 4.4 %collective-permute-done.1 = bf16[256,512]{0,1:T(8,128)(2,1)S(1)} collective-permute-done((bf16[256,512]{0,1:T(8,128)(2,1)S(1)}, bf16[256,512]{0,1:T(8,128)(2,1)S(1)}, u32[]{:S(2)}, u32[]{:S(2)}) %collective-permute-start.1) | collective-permute-done | bytes 262176 | tf_op jit(solution)/shard_map/while/body/eval_jaxpr/ppermute | solution.py:14
  78.1 20.4 %collective-permute-done.1 = bf16[256,512]{0,1:T(8,128)(2,1)S(1)} collective-permute-done((bf16[256,512]{0,1:T(8,128)(2,1)S(1)}, bf16[256,512]{0,1:T(8,128)(2,1)S(1)}, u32[]{:S(2)}, u32[]{:S(2)}) %collective-permute-start.1) | collective-permute-done | bytes 262176 | tf_op jit(solution)/shard_map/while/body/eval_jaxpr/ppermute | solution.py:14
  100.5 7.0 %collective-permute-done.2 = bf16[256,512]{0,1:T(8,128)(2,1)S(1)} collective-permute-done((bf16[256,512]{0,1:T(8,128)(2,1)S(1)}, bf16[256,512]{0,1:T(8,128)(2,1)S(1)}, u32[]{:S(2)}, u32[]{:S(2)}) %collective-permute-start.2) | collective-permute-done | bytes 262176 | tf_op jit(solution)/shard_map/while/body/eval_jaxpr/ppermute | solution.py:14
  107.5 1.9 bitcast_add_fusion.3
  116.7 11.2 %collective-permute-done.1 = bf16[256,512]{0,1:T(8,128)(2,1)S(1)} collective-permute-done((bf16[256,512]{0,1:T(8,128)(2,1)S(1)}, bf16[256,512]{0,1:T(8,128)(2,1)S(1)}, u32[]{:S(2)}, u32[]{:S(2)}) %collective-permute-start.1) | collective-permute-done | bytes 262176 | tf_op jit(solution)/shard_map/while/body/eval_jaxpr/ppermute | solution.py:14
  129.9 7.5 %collective-permute-done.2 = bf16[256,512]{0,1:T(8,128)(2,1)S(1)} collective-permute-done((bf16[256,512]{0,1:T(8,128)(2,1)S(1)}, bf16[256,512]{0,1:T(8,128)(2,1)S(1)}, u32[]{:S(2)}, u32[]{:S(2)}) %collective-permute-start.2) | collective-permute-done | bytes 262176 | tf_op jit(solution)/shard_map/while/body/eval_jaxpr/ppermute | solution.py:14
  146.6 8.7 %collective-permute-done.1 = bf16[256,512]{0,1:T(8,128)(2,1)S(1)} collective-permute-done((bf16[256,512]{0,1:T(8,128)(2,1)S(1)}, bf16[256,512]{0,1:T(8,128)(2,1)S(1)}, u32[]{:S(2)}, u32[]{:S(2)}) %collective-permute-start.1) | collective-permute-done | bytes 262176 | tf_op jit(solution)/shard_map/while/body/eval_jaxpr/ppermute | solution.py:14
  158.2 1.9 bitcast_add_fusion.3
  167.4 4.5 %collective-permute-done.1 = bf16[256,512]{0,1:T(8,128)(2,1)S(1)} collective-permute-done((bf16[256,512]{0,1:T(8,128)(2,1)S(1)}, bf16[256,512]{0,1:T(8,128)(2,1)S(1)}, u32[]{:S(2)}, u32[]{:S(2)}) %collective-permute-start.1) | collective-permute-done | bytes 262176 | tf_op jit(solution)/shard_map/while/body/eval_jaxpr/ppermute | solution.py:14
  174.7 1.9 bitcast_add_fusion.3
  184.0 4.5 %collective-permute-done.1 = bf16[256,512]{0,1:T(8,128)(2,1)S(1)} collective-permute-done((bf16[256,512]{0,1:T(8,128)(2,1)S(1)}, bf16[256,512]{0,1:T(8,128)(2,1)S(1)}, u32[]{:S(2)}, u32[]{:S(2)}) %collective-permute-start.1) | collective-permute-done | bytes 262176 | tf_op jit(solution)/shard_map/while/body/eval_jaxpr/ppermute | solution.py:14
  200.6 4.5 %collective-permute-done.1 = bf16[256,512]{0,1:T(8,128)(2,1)S(1)} collective-permute-done((bf16[256,512]{0,1:T(8,128)(2,1)S(1)}, bf16[256,512]{0,1:T(8,128)(2,1)S(1)}, u32[]{:S(2)}, u32[]{:S(2)}) %collective-permute-start.1) | collective-permute-done | bytes 262176 | tf_op jit(solution)/shard_map/while/body/eval_jaxpr/ppermute | solution.py:14
  217.1 4.5 %collective-permute-done.1 = bf16[256,512]{0,1:T(8,128)(2,1)S(1)} collective-permute-done((bf16[256,512]{0,1:T(8,128)(2,1)S(1)}, bf16[256,512]{0,1:T(8,128)(2,1)S(1)}, u32[]{:S(2)}, u32[]{:S(2)}) %collective-permute-start.1) | collective-permute-done | bytes 262176 | tf_op jit(solution)/shard_map/while/body/eval_jaxpr/ppermute | solution.py:14
  224.4 1.9 bitcast_add_fusion.3
  233.7 4.5 %collective-permute-done.1 = bf16[256,512]{0,1:T(8,128)(2,1)S(1)} collective-permute-done((bf16[256,512]{0,1:T(8,128)(2,1)S(1)}, bf16[256,512]{0,1:T(8,128)(2,1)S(1)}, u32[]{:S(2)}, u32[]{:S(2)}) %collective-permute-start.1) | collective-permute-done | bytes 262176 | tf_op jit(solution)/shard_map/while/body/eval_jaxpr/ppermute | solution.py:14
  241.0 1.9 bitcast_add_fusion.3
  250.3 4.5 %collective-permute-done.1 = bf16[256,512]{0,1:T(8,128)(2,1)S(1)} collective-permute-done((bf16[256,512]{0,1:T(8,128)(2,1)S(1)}, bf16[256,512]{0,1:T(8,128)(2,1)S(1)}, u32[]{:S(2)}, u32[]{:S(2)}) %collective-permute-start.1) | collective-permute-done | bytes 262176 | tf_op jit(solution)/shard_map/while/body/eval_jaxpr/ppermute | solution.py:14
  266.8 4.5 %collective-permute-done.1 = bf16[256,512]{0,1:T(8,128)(2,1)S(1)} collective-permute-done((bf16[256,512]{0,1:T(8,128)(2,1)S(1)}, bf16[256,512]{0,1:T(8,128)(2,1)S(1)}, u32[]{:S(2)}, u32[]{:S(2)}) %collective-permute-start.1) | collective-permute-done | bytes 262176 | tf_op jit(solution)/shard_map/while/body/eval_jaxpr/ppermute | solution.py:14
  283.4 4.5 %collective-permute-done.1 = bf16[256,512]{0,1:T(8,128)(2,1)S(1)} collective-permute-done((bf16[256,512]{0,1:T(8,128)(2,1)S(1)}, bf16[256,512]{0,1:T(8,128)(2,1)S(1)}, u32[]{:S(2)}, u32[]{:S(2)}) %collective-permute-start.1) | collective-permute-done | bytes 262176 | tf_op jit(solution)/shard_map/while/body/eval_jaxpr/ppermute | solution.py:14
  290.7 1.9 bitcast_add_fusion.3
  300.0 4.5 %collective-permute-done.1 = bf16[256,512]{0,1:T(8,128)(2,1)S(1)} collective-permute-done((bf16[256,512]{0,1:T(8,128)(2,1)S(1)}, bf16[256,512]{0,1:T(8,128)(2,1)S(1)}, u32[]{:S(2)}, u32[]{:S(2)}) %collective-permute-start.1) | collective-permute-done | bytes 262176 | tf_op jit(solution)/shard_map/while/body/eval_jaxpr/ppermute | solution.py:14
  307.3 1.9 bitcast_add_fusion.3
  316.6 4.5 %collective-permute-done.1 = bf16[256,512]{0,1:T(8,128)(2,1)S(1)} collective-permute-done((bf16[256,512]{0,1:T(8,128)(2,1)S(1)}, bf16[256,512]{0,1:T(8,128)(2,1)S(1)}, u32[]{:S(2)}, u32[]{:S(2)}) %collective-permute-start.1) | collective-permute-done | bytes 262176 | tf_op jit(solution)/shard_map/while/body/eval_jaxpr/ppermute | solution.py:14
  333.1 4.5 %collective-permute-done.1 = bf16[256,512]{0,1:T(8,128)(2,1)S(1)} collective-permute-done((bf16[256,512]{0,1:T(8,128)(2,1)S(1)}, bf16[256,512]{0,1:T(8,128)(2,1)S(1)}, u32[]{:S(2)}, u32[]{:S(2)}) %collective-permute-start.1) | collective-permute-done | bytes 262176 | tf_op jit(solution)/shard_map/while/body/eval_jaxpr/ppermute | solution.py:14
  345.9 11.6 %convolution_convert_fusion = bf16[256,4096]{1,0:T(8,128)(2,1)} fusion(bf16[256,2048]{0,1:T(8,128)(2,1)S(1)} %bitcast.91, bf16[2048,4096]{1,0:T(8,128)(2,1)} %all-gather.2.cloned.1.call-done), kind=kOutput, calls=%fused_computation.25 | convolution fusion | flops 4296015872 | bytes 19922944 | tf_op jit(solution)/shard_map/dot_general | solution.py:81
  357.4 32.0 %reduce-scatter.2.cloned.1.call-done = bf16[256,2048]{1,0:T(8,128)(2,1)} async-done(((bf16[256,4096]{1,0:T(8,128)(2,1)}), bf16[256,2048]{1,0:T(8,128)(2,1)}) %reduce-scatter.2.cloned.1.call-update) | async-done | bytes 1048592 | tf_op jit(solution)/shard_map/reduce_scatter | solution.py:86
  (349 shorter events, 184.8 us)
Async XLA Ops:
  6.5 339.3 %all-gather.2.cloned.1.call-start = ((), (), s32[]{:S(2)}) async-start(), calls=%async_computation.1 | async-start | bytes 17825792 | tf_op jit(solution)/shard_map/all_gather | solution.py:83
  7.3 382.2 %reduce-scatter.2.cloned.1.call-start = ((), (), s32[]{:S(2)}) async-start(), calls=%async_computation.2 | async-start | bytes 3145728 | tf_op jit(solution)/shard_map/reduce_scatter | solution.py:86
  25.4 13.3 %collective-permute-start.1 = (bf16[256,512]{0,1:T(8,128)(2,1)S(1)}, bf16[256,512]{0,1:T(8,128)(2,1)S(1)}, u32[]{:S(2)}, u32[]{:S(2)}) collective-permute-start(bf16[256,512]{0,1:T(8,128)(2,1)S(1)} %get-tuple-element.360), channel_id=1, source_target_pairs={{0,1},{1,2},{2,3},{3,4},{4,5},{5,6},{6,7},{7,8},{8,9},{9,10},{10,1... | collective-permute-start | bytes 786440 | tf_op jit(solution)/shard_map/while/body/eval_jaxpr/ppermute | solution.py:14
  28.9 23.3 %collective-permute-start.2 = (bf16[256,512]{0,1:T(8,128)(2,1)S(1)}, bf16[256,512]{0,1:T(8,128)(2,1)S(1)}, u32[]{:S(2)}, u32[]{:S(2)}) collective-permute-start(bf16[256,512]{0,1:T(8,128)(2,1)S(1)} %get-tuple-element.361), channel_id=1, source_target_pairs={{0,1},{1,2},{2,3},{3,4},{4,5},{5,6},{6,7},{7,8},{8,9},{9,10},{10,1... | collective-permute-start | bytes 786440 | tf_op jit(solution)/shard_map/while/body/eval_jaxpr/ppermute | solution.py:14
  57.4 8.6 %collective-permute-start.1 = (bf16[256,512]{0,1:T(8,128)(2,1)S(1)}, bf16[256,512]{0,1:T(8,128)(2,1)S(1)}, u32[]{:S(2)}, u32[]{:S(2)}) collective-permute-start(bf16[256,512]{0,1:T(8,128)(2,1)S(1)} %get-tuple-element.360), channel_id=1, source_target_pairs={{0,1},{1,2},{2,3},{3,4},{4,5},{5,6},{6,7},{7,8},{8,9},{9,10},{10,1... | collective-permute-start | bytes 786440 | tf_op jit(solution)/shard_map/while/body/eval_jaxpr/ppermute | solution.py:14
  59.3 9.5 %collective-permute-start.2 = (bf16[256,512]{0,1:T(8,128)(2,1)S(1)}, bf16[256,512]{0,1:T(8,128)(2,1)S(1)}, u32[]{:S(2)}, u32[]{:S(2)}) collective-permute-start(bf16[256,512]{0,1:T(8,128)(2,1)S(1)} %get-tuple-element.361), channel_id=1, source_target_pairs={{0,1},{1,2},{2,3},{3,4},{4,5},{5,6},{6,7},{7,8},{8,9},{9,10},{10,1... | collective-permute-start | bytes 786440 | tf_op jit(solution)/shard_map/while/body/eval_jaxpr/ppermute | solution.py:14
  74.0 24.6 %collective-permute-start.1 = (bf16[256,512]{0,1:T(8,128)(2,1)S(1)}, bf16[256,512]{0,1:T(8,128)(2,1)S(1)}, u32[]{:S(2)}, u32[]{:S(2)}) collective-permute-start(bf16[256,512]{0,1:T(8,128)(2,1)S(1)} %get-tuple-element.360), channel_id=1, source_target_pairs={{0,1},{1,2},{2,3},{3,4},{4,5},{5,6},{6,7},{7,8},{8,9},{9,10},{10,1... | collective-permute-start | bytes 786440 | tf_op jit(solution)/shard_map/while/body/eval_jaxpr/ppermute | solution.py:14
  75.9 31.6 %collective-permute-start.2 = (bf16[256,512]{0,1:T(8,128)(2,1)S(1)}, bf16[256,512]{0,1:T(8,128)(2,1)S(1)}, u32[]{:S(2)}, u32[]{:S(2)}) collective-permute-start(bf16[256,512]{0,1:T(8,128)(2,1)S(1)} %get-tuple-element.361), channel_id=1, source_target_pairs={{0,1},{1,2},{2,3},{3,4},{4,5},{5,6},{6,7},{7,8},{8,9},{9,10},{10,1... | collective-permute-start | bytes 786440 | tf_op jit(solution)/shard_map/while/body/eval_jaxpr/ppermute | solution.py:14
  112.7 15.2 %collective-permute-start.1 = (bf16[256,512]{0,1:T(8,128)(2,1)S(1)}, bf16[256,512]{0,1:T(8,128)(2,1)S(1)}, u32[]{:S(2)}, u32[]{:S(2)}) collective-permute-start(bf16[256,512]{0,1:T(8,128)(2,1)S(1)} %get-tuple-element.360), channel_id=1, source_target_pairs={{0,1},{1,2},{2,3},{3,4},{4,5},{5,6},{6,7},{7,8},{8,9},{9,10},{10,1... | collective-permute-start | bytes 786440 | tf_op jit(solution)/shard_map/while/body/eval_jaxpr/ppermute | solution.py:14
  114.6 22.8 %collective-permute-start.2 = (bf16[256,512]{0,1:T(8,128)(2,1)S(1)}, bf16[256,512]{0,1:T(8,128)(2,1)S(1)}, u32[]{:S(2)}, u32[]{:S(2)}) collective-permute-start(bf16[256,512]{0,1:T(8,128)(2,1)S(1)} %get-tuple-element.361), channel_id=1, source_target_pairs={{0,1},{1,2},{2,3},{3,4},{4,5},{5,6},{6,7},{7,8},{8,9},{9,10},{10,1... | collective-permute-start | bytes 786440 | tf_op jit(solution)/shard_map/while/body/eval_jaxpr/ppermute | solution.py:14
  142.5 12.8 %collective-permute-start.1 = (bf16[256,512]{0,1:T(8,128)(2,1)S(1)}, bf16[256,512]{0,1:T(8,128)(2,1)S(1)}, u32[]{:S(2)}, u32[]{:S(2)}) collective-permute-start(bf16[256,512]{0,1:T(8,128)(2,1)S(1)} %get-tuple-element.360), channel_id=1, source_target_pairs={{0,1},{1,2},{2,3},{3,4},{4,5},{5,6},{6,7},{7,8},{8,9},{9,10},{10,1... | collective-permute-start | bytes 786440 | tf_op jit(solution)/shard_map/while/body/eval_jaxpr/ppermute | solution.py:14
  144.5 13.7 %collective-permute-start.2 = (bf16[256,512]{0,1:T(8,128)(2,1)S(1)}, bf16[256,512]{0,1:T(8,128)(2,1)S(1)}, u32[]{:S(2)}, u32[]{:S(2)}) collective-permute-start(bf16[256,512]{0,1:T(8,128)(2,1)S(1)} %get-tuple-element.361), channel_id=1, source_target_pairs={{0,1},{1,2},{2,3},{3,4},{4,5},{5,6},{6,7},{7,8},{8,9},{9,10},{10,1... | collective-permute-start | bytes 786440 | tf_op jit(solution)/shard_map/while/body/eval_jaxpr/ppermute | solution.py:14
  163.3 8.6 %collective-permute-start.1 = (bf16[256,512]{0,1:T(8,128)(2,1)S(1)}, bf16[256,512]{0,1:T(8,128)(2,1)S(1)}, u32[]{:S(2)}, u32[]{:S(2)}) collective-permute-start(bf16[256,512]{0,1:T(8,128)(2,1)S(1)} %get-tuple-element.360), channel_id=1, source_target_pairs={{0,1},{1,2},{2,3},{3,4},{4,5},{5,6},{6,7},{7,8},{8,9},{9,10},{10,1... | collective-permute-start | bytes 786440 | tf_op jit(solution)/shard_map/while/body/eval_jaxpr/ppermute | solution.py:14
  165.3 9.5 %collective-permute-start.2 = (bf16[256,512]{0,1:T(8,128)(2,1)S(1)}, bf16[256,512]{0,1:T(8,128)(2,1)S(1)}, u32[]{:S(2)}, u32[]{:S(2)}) collective-permute-start(bf16[256,512]{0,1:T(8,128)(2,1)S(1)} %get-tuple-element.361), channel_id=1, source_target_pairs={{0,1},{1,2},{2,3},{3,4},{4,5},{5,6},{6,7},{7,8},{8,9},{9,10},{10,1... | collective-permute-start | bytes 786440 | tf_op jit(solution)/shard_map/while/body/eval_jaxpr/ppermute | solution.py:14
  179.9 8.6 %collective-permute-start.1 = (bf16[256,512]{0,1:T(8,128)(2,1)S(1)}, bf16[256,512]{0,1:T(8,128)(2,1)S(1)}, u32[]{:S(2)}, u32[]{:S(2)}) collective-permute-start(bf16[256,512]{0,1:T(8,128)(2,1)S(1)} %get-tuple-element.360), channel_id=1, source_target_pairs={{0,1},{1,2},{2,3},{3,4},{4,5},{5,6},{6,7},{7,8},{8,9},{9,10},{10,1... | collective-permute-start | bytes 786440 | tf_op jit(solution)/shard_map/while/body/eval_jaxpr/ppermute | solution.py:14
  181.8 9.5 %collective-permute-start.2 = (bf16[256,512]{0,1:T(8,128)(2,1)S(1)}, bf16[256,512]{0,1:T(8,128)(2,1)S(1)}, u32[]{:S(2)}, u32[]{:S(2)}) collective-permute-start(bf16[256,512]{0,1:T(8,128)(2,1)S(1)} %get-tuple-element.361), channel_id=1, source_target_pairs={{0,1},{1,2},{2,3},{3,4},{4,5},{5,6},{6,7},{7,8},{8,9},{9,10},{10,1... | collective-permute-start | bytes 786440 | tf_op jit(solution)/shard_map/while/body/eval_jaxpr/ppermute | solution.py:14
  196.5 8.6 %collective-permute-start.1 = (bf16[256,512]{0,1:T(8,128)(2,1)S(1)}, bf16[256,512]{0,1:T(8,128)(2,1)S(1)}, u32[]{:S(2)}, u32[]{:S(2)}) collective-permute-start(bf16[256,512]{0,1:T(8,128)(2,1)S(1)} %get-tuple-element.360), channel_id=1, source_target_pairs={{0,1},{1,2},{2,3},{3,4},{4,5},{5,6},{6,7},{7,8},{8,9},{9,10},{10,1... | collective-permute-start | bytes 786440 | tf_op jit(solution)/shard_map/while/body/eval_jaxpr/ppermute | solution.py:14
  198.4 9.5 %collective-permute-start.2 = (bf16[256,512]{0,1:T(8,128)(2,1)S(1)}, bf16[256,512]{0,1:T(8,128)(2,1)S(1)}, u32[]{:S(2)}, u32[]{:S(2)}) collective-permute-start(bf16[256,512]{0,1:T(8,128)(2,1)S(1)} %get-tuple-element.361), channel_id=1, source_target_pairs={{0,1},{1,2},{2,3},{3,4},{4,5},{5,6},{6,7},{7,8},{8,9},{9,10},{10,1... | collective-permute-start | bytes 786440 | tf_op jit(solution)/shard_map/while/body/eval_jaxpr/ppermute | solution.py:14
  213.0 8.6 %collective-permute-start.1 = (bf16[256,512]{0,1:T(8,128)(2,1)S(1)}, bf16[256,512]{0,1:T(8,128)(2,1)S(1)}, u32[]{:S(2)}, u32[]{:S(2)}) collective-permute-start(bf16[256,512]{0,1:T(8,128)(2,1)S(1)} %get-tuple-element.360), channel_id=1, source_target_pairs={{0,1},{1,2},{2,3},{3,4},{4,5},{5,6},{6,7},{7,8},{8,9},{9,10},{10,1... | collective-permute-start | bytes 786440 | tf_op jit(solution)/shard_map/while/body/eval_jaxpr/ppermute | solution.py:14
  215.0 9.5 %collective-permute-start.2 = (bf16[256,512]{0,1:T(8,128)(2,1)S(1)}, bf16[256,512]{0,1:T(8,128)(2,1)S(1)}, u32[]{:S(2)}, u32[]{:S(2)}) collective-permute-start(bf16[256,512]{0,1:T(8,128)(2,1)S(1)} %get-tuple-element.361), channel_id=1, source_target_pairs={{0,1},{1,2},{2,3},{3,4},{4,5},{5,6},{6,7},{7,8},{8,9},{9,10},{10,1... | collective-permute-start | bytes 786440 | tf_op jit(solution)/shard_map/while/body/eval_jaxpr/ppermute | solution.py:14
  229.6 8.6 %collective-permute-start.1 = (bf16[256,512]{0,1:T(8,128)(2,1)S(1)}, bf16[256,512]{0,1:T(8,128)(2,1)S(1)}, u32[]{:S(2)}, u32[]{:S(2)}) collective-permute-start(bf16[256,512]{0,1:T(8,128)(2,1)S(1)} %get-tuple-element.360), channel_id=1, source_target_pairs={{0,1},{1,2},{2,3},{3,4},{4,5},{5,6},{6,7},{7,8},{8,9},{9,10},{10,1... | collective-permute-start | bytes 786440 | tf_op jit(solution)/shard_map/while/body/eval_jaxpr/ppermute | solution.py:14
  231.5 9.5 %collective-permute-start.2 = (bf16[256,512]{0,1:T(8,128)(2,1)S(1)}, bf16[256,512]{0,1:T(8,128)(2,1)S(1)}, u32[]{:S(2)}, u32[]{:S(2)}) collective-permute-start(bf16[256,512]{0,1:T(8,128)(2,1)S(1)} %get-tuple-element.361), channel_id=1, source_target_pairs={{0,1},{1,2},{2,3},{3,4},{4,5},{5,6},{6,7},{7,8},{8,9},{9,10},{10,1... | collective-permute-start | bytes 786440 | tf_op jit(solution)/shard_map/while/body/eval_jaxpr/ppermute | solution.py:14
  246.2 8.6 %collective-permute-start.1 = (bf16[256,512]{0,1:T(8,128)(2,1)S(1)}, bf16[256,512]{0,1:T(8,128)(2,1)S(1)}, u32[]{:S(2)}, u32[]{:S(2)}) collective-permute-start(bf16[256,512]{0,1:T(8,128)(2,1)S(1)} %get-tuple-element.360), channel_id=1, source_target_pairs={{0,1},{1,2},{2,3},{3,4},{4,5},{5,6},{6,7},{7,8},{8,9},{9,10},{10,1... | collective-permute-start | bytes 786440 | tf_op jit(solution)/shard_map/while/body/eval_jaxpr/ppermute | solution.py:14
  248.1 9.5 %collective-permute-start.2 = (bf16[256,512]{0,1:T(8,128)(2,1)S(1)}, bf16[256,512]{0,1:T(8,128)(2,1)S(1)}, u32[]{:S(2)}, u32[]{:S(2)}) collective-permute-start(bf16[256,512]{0,1:T(8,128)(2,1)S(1)} %get-tuple-element.361), channel_id=1, source_target_pairs={{0,1},{1,2},{2,3},{3,4},{4,5},{5,6},{6,7},{7,8},{8,9},{9,10},{10,1... | collective-permute-start | bytes 786440 | tf_op jit(solution)/shard_map/while/body/eval_jaxpr/ppermute | solution.py:14
  262.8 8.6 %collective-permute-start.1 = (bf16[256,512]{0,1:T(8,128)(2,1)S(1)}, bf16[256,512]{0,1:T(8,128)(2,1)S(1)}, u32[]{:S(2)}, u32[]{:S(2)}) collective-permute-start(bf16[256,512]{0,1:T(8,128)(2,1)S(1)} %get-tuple-element.360), channel_id=1, source_target_pairs={{0,1},{1,2},{2,3},{3,4},{4,5},{5,6},{6,7},{7,8},{8,9},{9,10},{10,1... | collective-permute-start | bytes 786440 | tf_op jit(solution)/shard_map/while/body/eval_jaxpr/ppermute | solution.py:14
  264.7 9.5 %collective-permute-start.2 = (bf16[256,512]{0,1:T(8,128)(2,1)S(1)}, bf16[256,512]{0,1:T(8,128)(2,1)S(1)}, u32[]{:S(2)}, u32[]{:S(2)}) collective-permute-start(bf16[256,512]{0,1:T(8,128)(2,1)S(1)} %get-tuple-element.361), channel_id=1, source_target_pairs={{0,1},{1,2},{2,3},{3,4},{4,5},{5,6},{6,7},{7,8},{8,9},{9,10},{10,1... | collective-permute-start | bytes 786440 | tf_op jit(solution)/shard_map/while/body/eval_jaxpr/ppermute | solution.py:14
  279.3 8.6 %collective-permute-start.1 = (bf16[256,512]{0,1:T(8,128)(2,1)S(1)}, bf16[256,512]{0,1:T(8,128)(2,1)S(1)}, u32[]{:S(2)}, u32[]{:S(2)}) collective-permute-start(bf16[256,512]{0,1:T(8,128)(2,1)S(1)} %get-tuple-element.360), channel_id=1, source_target_pairs={{0,1},{1,2},{2,3},{3,4},{4,5},{5,6},{6,7},{7,8},{8,9},{9,10},{10,1... | collective-permute-start | bytes 786440 | tf_op jit(solution)/shard_map/while/body/eval_jaxpr/ppermute | solution.py:14
  281.3 9.5 %collective-permute-start.2 = (bf16[256,512]{0,1:T(8,128)(2,1)S(1)}, bf16[256,512]{0,1:T(8,128)(2,1)S(1)}, u32[]{:S(2)}, u32[]{:S(2)}) collective-permute-start(bf16[256,512]{0,1:T(8,128)(2,1)S(1)} %get-tuple-element.361), channel_id=1, source_target_pairs={{0,1},{1,2},{2,3},{3,4},{4,5},{5,6},{6,7},{7,8},{8,9},{9,10},{10,1... | collective-permute-start | bytes 786440 | tf_op jit(solution)/shard_map/while/body/eval_jaxpr/ppermute | solution.py:14
  295.9 8.6 %collective-permute-start.1 = (bf16[256,512]{0,1:T(8,128)(2,1)S(1)}, bf16[256,512]{0,1:T(8,128)(2,1)S(1)}, u32[]{:S(2)}, u32[]{:S(2)}) collective-permute-start(bf16[256,512]{0,1:T(8,128)(2,1)S(1)} %get-tuple-element.360), channel_id=1, source_target_pairs={{0,1},{1,2},{2,3},{3,4},{4,5},{5,6},{6,7},{7,8},{8,9},{9,10},{10,1... | collective-permute-start | bytes 786440 | tf_op jit(solution)/shard_map/while/body/eval_jaxpr/ppermute | solution.py:14
  297.8 9.5 %collective-permute-start.2 = (bf16[256,512]{0,1:T(8,128)(2,1)S(1)}, bf16[256,512]{0,1:T(8,128)(2,1)S(1)}, u32[]{:S(2)}, u32[]{:S(2)}) collective-permute-start(bf16[256,512]{0,1:T(8,128)(2,1)S(1)} %get-tuple-element.361), channel_id=1, source_target_pairs={{0,1},{1,2},{2,3},{3,4},{4,5},{5,6},{6,7},{7,8},{8,9},{9,10},{10,1... | collective-permute-start | bytes 786440 | tf_op jit(solution)/shard_map/while/body/eval_jaxpr/ppermute | solution.py:14
  314.4 9.5 %collective-permute-start.2 = (bf16[256,512]{0,1:T(8,128)(2,1)S(1)}, bf16[256,512]{0,1:T(8,128)(2,1)S(1)}, u32[]{:S(2)}, u32[]{:S(2)}) collective-permute-start(bf16[256,512]{0,1:T(8,128)(2,1)S(1)} %get-tuple-element.361), channel_id=1, source_target_pairs={{0,1},{1,2},{2,3},{3,4},{4,5},{5,6},{6,7},{7,8},{8,9},{9,10},{10,1... | collective-permute-start | bytes 786440 | tf_op jit(solution)/shard_map/while/body/eval_jaxpr/ppermute | solution.py:14
  331.0 9.5 %collective-permute-start.2 = (bf16[256,512]{0,1:T(8,128)(2,1)S(1)}, bf16[256,512]{0,1:T(8,128)(2,1)S(1)}, u32[]{:S(2)}, u32[]{:S(2)}) collective-permute-start(bf16[256,512]{0,1:T(8,128)(2,1)S(1)} %get-tuple-element.361), channel_id=1, source_target_pairs={{0,1},{1,2},{2,3},{3,4},{4,5},{5,6},{6,7},{7,8},{8,9},{9,10},{10,1... | collective-permute-start | bytes 786440 | tf_op jit(solution)/shard_map/while/body/eval_jaxpr/ppermute | solution.py:14
  (52 other events, 210.7 us)
Sparse Core Ops, SparseCore 0:
  9.5 145.3 all-gather.1
  357.6 31.8 reduce-scatter.1
where the time goes:
time: 400 us; the launch traced here: 396 us
  waiting for transfers between devices  172 us (43%)
  starting transfers between devices  93.6 us (23%)
  matrix products  63 us (16%)
  local copies, waits for them, and re-layouts  31.1 us (8%)
  other arithmetic  21.2 us (5%)
  between operations  13.5 us (3%)
    ppermute x48, waiting for transfers between devices, passed_along(): return lax.ppermute(block, axis, route)  139 us
    ppermute x48, starting transfers between devices, passed_along(): return lax.ppermute(block, axis, route)  93.6 us
    dot_general x17, matrix products, work(): jnp.einsum('tgns,sgh->tgnh', rounded, vblk.reshape(tok_rows, groups, HEAD...  36.5 us
    reduce_scatter x1, waiting for transfers between devices, body(): lax.psum_scatter(partial_sums.astype(jnp.bfloat16), 'heads', scatter_dime...  32 us
    while x128, local copies, waits for them, and re-layouts  20.9 us
    reduce_sum x17, other arithmetic, work(): total = total * factor + jnp.sum(weights, axis=-1)  17.6 us
    dot_general x17, matrix products, work(): jnp.einsum('tgnh,sgh->tgns', q_local, kblk.reshape(tok_rows, groups, HEAD...  15 us
    dot_general x1, matrix products, body(): jnp.dot(attn, lax.all_gather(out_weight, 'ctx', axis=1, tiled=True), pref...  11.6 us
  transfers between devices with their start and end apart: 50, of which 35 were waited for; matrix products, arithmetic and copies ran while one was open for 21% of the time, Pallas kernels for 0%

commit v1 on v0

--- a/solution.py
+++ b/solution.py
@@ -1,11 +1,535 @@
+import functools
+import math
+
 import jax
 import jax.numpy as jnp
 from jax import lax
+from jax.experimental import pallas as pl
+from jax.experimental.pallas import tpu as pltpu
 from jax.sharding import PartitionSpec as P
 
 HEAD_SIZE = 128
 LOOKBACK_WINDOW = 4096
 QPG = 4
+
+
+PLANE = 4
+DOC_ROWS = 16
+MESH = pl.DeviceIdType.MESH
+
+
+def fused_kernel(
+    planes, n_heads, groups, tok, wcols,
+    q_ref, kv_hbm, w_hbm, out_ref,
+    kvbuf, wbuf, abuf, acc, rowmax, total, bias, xsend, xrecv, keep, rsend, obuf,
+    local_sem, kv_recv, kvz_send, kvp_send, kvf_send,
+    w_recv, w_right, w_left, a_recv, a_send, a_fwd,
+    x_send, x_recv, o_send, o_recv,
+):
+    h = lax.axis_index("heads")
+    c = lax.axis_index("ctx")
+    z = c // PLANE
+    p = c % PLANE
+    core = p % 2
+    row = p // 2
+    mate = p + 1 - 2 * core
+    across = (p + 2) % PLANE
+    diag = (mate + 2) % PLANE
+    last = planes - 1
+    kdim = groups * HEAD_SIZE
+    span = QPG * groups
+    per_half = planes // n_heads
+
+    def in_plane(other):
+        return (h, z * PLANE + other)
+
+    up = (h, c + PLANE)
+    down = (h, c - PLANE)
+
+    def copy(src, dst, send, recv, dev):
+        return pltpu.make_async_remote_copy(
+            src_ref=src, dst_ref=dst, send_sem=send, recv_sem=recv,
+            device_id=dev, device_id_type=MESH,
+        )
+
+    def kv_up(d):
+        return copy(kvbuf.at[d, p], kvbuf.at[d + 1, p], kvz_send.at[d], kv_recv.at[d + 1, p], up)
+
+    def kv_side(d, which):
+        dev = in_plane(mate if which == 0 else across)
+        return copy(kvbuf.at[d, p], kvbuf.at[d, p], kvp_send.at[d, which], kv_recv.at[d, p], dev)
+
+    def kv_forward(d):
+        return copy(
+            kvbuf.at[d, across], kvbuf.at[d, across], kvf_send.at[d], kv_recv.at[d, across],
+            in_plane(mate),
+        )
+
+    def kv_wait(d, who):
+        copy(
+            kvbuf.at[d, who], kvbuf.at[d, who], kvf_send.at[d], kv_recv.at[d, who], in_plane(mate)
+        ).wait_recv()
+
+    def w_up(j):
+        return copy(wbuf.at[j], wbuf.at[j], w_right.at[j], w_recv.at[j], up)
+
+    def w_down(j):
+        return copy(wbuf.at[j], wbuf.at[j], w_left.at[j], w_recv.at[j], down)
+
+    def w_wait(j):
+        copy(wbuf.at[j], wbuf.at[j], w_left.at[j], w_recv.at[j], in_plane(mate)).wait_recv()
+
+    def a_side(which):
+        dev = in_plane(mate if which == 0 else across)
+        return copy(abuf.at[p], abuf.at[p], a_send.at[which], a_recv.at[p], dev)
+
+    def a_forward():
+        return copy(abuf.at[across], abuf.at[across], a_fwd, a_recv.at[across], in_plane(mate))
+
+    def a_wait(who):
+        copy(abuf.at[who], abuf.at[who], a_fwd, a_recv.at[who], in_plane(mate)).wait_recv()
+
+    def x_copy(jj, pp):
+        return copy(
+            xsend.at[jj, pp], xrecv.at[jj, pp], x_send.at[jj, pp], x_recv.at[jj, pp], (1 - h, c)
+        )
+
+    def o_copy(jj, pp):
+        return copy(
+            rsend.at[jj, pp], obuf.at[jj, p], o_send.at[jj, pp], o_recv.at[jj, p], in_plane(pp)
+        )
+
+    kv_in = pltpu.make_async_copy(kv_hbm, kvbuf.at[0, p], local_sem.at[0])
+    w_in = pltpu.make_async_copy(w_hbm, wbuf.at[z], local_sem.at[1])
+    kv_in.start()
+    w_in.start()
+
+    barrier = pltpu.get_barrier_semaphore()
+    for dev in (in_plane(mate), in_plane(across), in_plane(diag), (1 - h, c)):
+        pl.semaphore_signal(barrier, inc=1, device_id=dev, device_id_type=MESH)
+
+    @pl.when(z < last)
+    def _():
+        pl.semaphore_signal(barrier, inc=1, device_id=up, device_id_type=MESH)
+
+    @pl.when(z > 0)
+    def _():
+        pl.semaphore_signal(barrier, inc=1, device_id=down, device_id_type=MESH)
+
+    pl.semaphore_wait(barrier, 4 + jnp.minimum(z, 1) + jnp.minimum(last - z, 1))
+
+    kv_in.wait()
+
+    @pl.when(z < last)
+    def _():
+        kv_up(0).start()
+
+    @pl.when(row == 0)
+    def _():
+        kv_side(0, 1).start()
+
+    @pl.when(core == 0)
+    def _():
+        kv_side(0, 0).start()
+
+    w_in.wait()
+
+    @pl.when(z > 0)
+    def _():
+        w_down(z).start()
+
+    factor = HEAD_SIZE ** (-0.5) * math.log2(math.e)
+
+    def docs_of(block):
+        return block[tok : tok + DOC_ROWS, 0:tok].astype(jnp.float32)[0:1, :]
+
+    def attend(d, who, first):
+        block = kvbuf.at[d, who]
+        kdoc = jnp.broadcast_to(docs_of(block), (tok, tok)).T
+        vis = kdoc == docs_of(kvbuf.at[0, p])
+        if first:
+            kpos = lax.broadcasted_iota(jnp.int32, (tok, tok), 0)
+            qpos = lax.broadcasted_iota(jnp.int32, (tok, tok), 1)
+            vis = vis & (kpos <= qpos)
+        bias[...] = jnp.where(vis, jnp.float32(0.0), jnp.float32(-1e30))
+
+        def group(g, carry):
+            keys = block[0:tok, pl.ds(pl.multiple_of(g * HEAD_SIZE, HEAD_SIZE), HEAD_SIZE)]
+            vals = block[0:tok, pl.ds(pl.multiple_of(kdim + g * HEAD_SIZE, HEAD_SIZE), HEAD_SIZE)]
+            for n in range(QPG):
+                head = g * QPG + n
+                qs = q_ref[:, pl.ds(pl.multiple_of(head * HEAD_SIZE, HEAD_SIZE), HEAD_SIZE)]
+                scores = lax.dot_general(
+                    keys, qs, (((1,), (1,)), ((), ())), preferred_element_type=jnp.float32
+                ) + bias[...]
+                top = jnp.max(scores, axis=0, keepdims=True)
+                if not first:
+                    old = rowmax[head]
+                    top = jnp.maximum(old, top)
+                weights = jnp.exp2((scores - top) * factor)
+                sums = jnp.sum(weights, axis=0, keepdims=True)
+                contrib = lax.dot_general(
+                    vals, weights.astype(jnp.bfloat16), (((0,), (0,)), ((), ())),
+                    preferred_element_type=jnp.float32,
+                )
+                if first:
+                    total[head] = sums
+                    acc[head] = contrib
+                else:
+                    shrink = jnp.exp2((old - top) * factor)
+                    total[head] = total[head] * shrink + sums
+                    acc[head] = acc[head] * shrink + contrib
+                rowmax[head] = top
+            return carry
+
+        lax.fori_loop(0, groups, group, 0)
+
+    attend(0, p, True)
+
+    @pl.when(z > 0)
+    def _():
+        kv_wait(1, p)
+
+        @pl.when(z < last)
+        def _():
+            kv_up(1).start()
+
+        kv_side(1, 1).start()
+        kv_side(1, 0).start()
+
+    @pl.when(z < last)
+    def _():
+        w_up(z).start()
+
+    @pl.when(row == 1)
+    def _():
+        kv_wait(0, across)
+        kv_forward(0).start()
+
+    @pl.when(core == 1)
+    def _():
+        kv_wait(0, mate)
+
+    @pl.when(row == 1)
+    def _():
+        kv_wait(0, diag)
+
+    def block_loop(d, lo, hi):
+        def one(who, carry):
+            attend(d, who, False)
+            return carry
+
+        lax.fori_loop(lo, hi, one, 0)
+
+    block_loop(0, 0, p)
+
+    @pl.when(z > 0)
+    def _():
+        kv_wait(1, across)
+        kv_forward(1).start()
+
+    @pl.when(z > 1)
+    def _():
+        kv_wait(2, p)
+
+        @pl.when(row == 1)
+        def _():
+            kv_side(2, 1).start()
+
+        @pl.when(core == 1)
+        def _():
+            kv_side(2, 0).start()
+
+    @pl.when(z < last)
+    def _():
+        w_wait(z + 1)
+
+        @pl.when(z > 0)
+        def _():
+            w_down(z + 1).start()
+
+    @pl.when(z > 0)
+    def _():
+        kv_wait(1, mate)
+        kv_wait(1, diag)
+        block_loop(1, 0, PLANE)
+
+    @pl.when(z > 1)
+    def _():
+        @pl.when(row == 0)
+        def _():
+            kv_wait(2, across)
+            kv_forward(2).start()
+
+        @pl.when(core == 0)
+        def _():
+            kv_wait(2, mate)
+
+        @pl.when(row == 0)
+        def _():
+            kv_wait(2, diag)
+
+        block_loop(2, p, PLANE)
+
+    def finish_head(head, carry):
+        cols = pl.ds(pl.multiple_of(head * HEAD_SIZE, HEAD_SIZE), HEAD_SIZE)
+        abuf[p, :, cols] = (acc[head] / total[head]).T.astype(jnp.bfloat16)
+        return carry
+
+    lax.fori_loop(0, span, finish_head, 0)
+    a_side(1).start()
+    a_side(0).start()
+
+    @pl.when(z > 0)
+    def _():
+        w_wait(z - 1)
+
+        @pl.when(z < last)
+        def _():
+            w_up(z - 1).start()
+
+    @pl.when(z + 2 < planes)
+    def _():
+        w_wait(z + 2)
+
+        @pl.when(z > 0)
+        def _():
+            w_down(z + 2).start()
+
+    a_wait(across)
+    a_forward().start()
+    a_wait(mate)
+    a_wait(diag)
+
+    def plane_of(i):
+        dist = (i + 1) // 2
+        return z + dist * (2 * (i % 2) - 1)
+
+    def project(i):
+        j = plane_of(i)
+
+        @pl.when((j >= 0) & (j < planes))
+        def _():
+            @pl.when(i >= 4)
+            def _():
+                w_wait(j)
+
+                @pl.when((j < z) & (z < last))
+                def _():
+                    w_up(j).start()
+
+                @pl.when((j > z) & (z > 0))
+                def _():
+                    w_down(j).start()
+
+            jj = j % per_half
+            mine = (j // per_half) == h
+
+            def rows(k, carry):
+                pp = (p + 1 + k) % PLANE
+                part = jnp.dot(abuf[pp], wbuf[j], preferred_element_type=jnp.float32)
+
+                @pl.when(mine)
+                def _():
+                    keep[jj, pp] = part
+
+                @pl.when(jnp.logical_not(mine))
+                def _():
+                    xsend[jj, pp] = part.astype(jnp.bfloat16)
+                    x_copy(jj, pp).start()
+
+                return carry
+
+            lax.fori_loop(0, PLANE, rows, 0)
+
+    def finish(i):
+        j = plane_of(i)
+
+        @pl.when((j >= 0) & (j < planes) & ((j // per_half) == h))
+        def _():
+            jj = j % per_half
+
+            def rows(k, carry):
+                pp = (p + 1 + k) % PLANE
+                x_copy(jj, pp).wait_recv()
+                done = (keep[jj, pp] + xrecv[jj, pp].astype(jnp.float32)).astype(jnp.bfloat16)
+
+                @pl.when(pp == p)
+                def _():
+                    at = pl.multiple_of((jj * PLANE + p) * wcols, wcols)
+                    out_ref[:, pl.ds(at, wcols)] = done
+
+                @pl.when(pp != p)
+                def _():
+                    rsend[jj, pp] = done
+                    o_copy(jj, pp).start()
+
+                return carry
+
+            lax.fori_loop(0, PLANE, rows, 0)
+
+    steps = 2 * planes - 1
+    project(0)
+
+    def step(i, carry):
+        project(i)
+        finish(i - 1)
+        return carry
+
+    lax.fori_loop(1, steps, step, 0)
+    finish(steps - 1)
+
+    def collect(k, carry):
+        jj = k // PLANE
+        src = k % PLANE
+
+        @pl.when(src != p)
+        def _():
+            copy(
+                obuf.at[jj, src], obuf.at[jj, src], o_send.at[jj, src], o_recv.at[jj, src],
+                in_plane(mate),
+            ).wait_recv()
+            at = pl.multiple_of(k * wcols, wcols)
+            out_ref[:, pl.ds(at, wcols)] = obuf[jj, src]
+            o_copy(jj, src).wait_send()
+
+        x_copy(jj, src).wait_send()
+        return carry
+
+    lax.fori_loop(0, per_half * PLANE, collect, 0)
+
+    a_side(0).wait_send()
+    a_side(1).wait_send()
+    a_forward().wait_send()
+
+    def w_drain(j, carry):
+        @pl.when((j <= z) & (z < last))
+        def _():
+            w_up(j).wait_send()
+
+        @pl.when((j >= z) & (z > 0))
+        def _():
+            w_down(j).wait_send()
+
+        return carry
+
+    lax.fori_loop(0, planes, w_drain, 0)
+
+    @pl.when(z < last)
+    def _():
+        kv_up(0).wait_send()
+
+        @pl.when(z > 0)
+        def _():
+            kv_up(1).wait_send()
+
+    @pl.when(row == 0)
+    def _():
+        kv_side(0, 1).wait_send()
+
+    @pl.when(core == 0)
+    def _():
+        kv_side(0, 0).wait_send()
+
+    @pl.when(row == 1)
+    def _():
+        kv_forward(0).wait_send()
+
+    @pl.when(z > 0)
+    def _():
+        kv_side(1, 0).wait_send()
+        kv_side(1, 1).wait_send()
+        kv_forward(1).wait_send()
+
+    @pl.when(z > 1)
+    def _():
+        @pl.when(row == 1)
+        def _():
+            kv_side(2, 1).wait_send()
+
+        @pl.when(core == 1)
+        def _():
+            kv_side(2, 0).wait_send()
+
+        @pl.when(row == 0)
+        def _():
+            kv_forward(2).wait_send()
+
+
+def fused_body(n_ctx, n_heads, queries, keys, values, doc_ids, out_weight):
+    tok, qcols = queries.shape
+    kdim = keys.shape[1]
+    groups = kdim // HEAD_SIZE
+    krows, wcols = out_weight.shape
+    planes = n_ctx // PLANE
+    span = QPG * groups
+    per_half = planes // n_heads
+    width = 2 * kdim
+    docs = jnp.broadcast_to(
+        jnp.pad(doc_ids.astype(jnp.bfloat16), (0, width - tok))[None, :], (DOC_ROWS, width)
+    )
+    kv = jnp.concatenate([jnp.concatenate([keys, values], axis=1), docs], axis=0)
+    bf, f32 = jnp.bfloat16, jnp.float32
+    dma = pltpu.SemaphoreType.DMA
+    return pl.pallas_call(
+        functools.partial(fused_kernel, planes, n_heads, groups, tok, wcols),
+        out_shape=jax.ShapeDtypeStruct((tok, per_half * PLANE * wcols), bf),
+        in_specs=[
+            pl.BlockSpec(memory_space=pltpu.VMEM),
+            pl.BlockSpec(memory_space=pl.ANY),
+            pl.BlockSpec(memory_space=pl.ANY),
+        ],
+        out_specs=pl.BlockSpec(memory_space=pltpu.VMEM),
+        scratch_shapes=[
+            pltpu.VMEM((3, PLANE, tok + DOC_ROWS, width), bf),
+            pltpu.VMEM((planes, krows, wcols), bf),
+            pltpu.VMEM((PLANE, tok, krows), bf),
+            pltpu.VMEM((span, HEAD_SIZE, tok), f32),
+            pltpu.VMEM((span, 1, tok), f32),
+            pltpu.VMEM((span, 1, tok), f32),
+            pltpu.VMEM((tok, tok), f32),
+            pltpu.VMEM((per_half, PLANE, tok, wcols), bf),
+            pltpu.VMEM((per_half, PLANE, tok, wcols), bf),
+            pltpu.VMEM((per_half, PLANE, tok, wcols), f32),
+            pltpu.VMEM((per_half, PLANE, tok, wcols), bf),
+            pltpu.VMEM((per_half, PLANE, tok, wcols), bf),
+            dma((2,)),
+            dma((3, PLANE)),
+            dma((2,)),
+            dma((3, 2)),
+            dma((3,)),
+            dma((planes,)),
+            dma((planes,)),
+            dma((planes,)),
+            dma((PLANE,)),
+            dma((2,)),
+            dma,
+            dma((per_half, PLANE)),
+            dma((per_half, PLANE)),
+            dma((per_half, PLANE)),
+            dma((per_half, PLANE)),
+        ],
+        compiler_params=pltpu.CompilerParams(
+            collective_id=0, has_side_effects=True, vmem_limit_bytes=56 * 1024 * 1024
+        ),
+    )(queries, kv, out_weight)
+
+
+def fits_fused(n_ctx, n_heads, queries, keys, out_weight):
+    tokens = queries.shape[0]
+    tok = tokens // n_ctx
+    reach = min(LOOKBACK_WINDOW, tokens // 2)
+    return (
+        n_heads == 2
+        and n_ctx % PLANE == 0
+        and n_ctx // PLANE == 4
+        and tok == 2 * HEAD_SIZE
+        and reach == 2 * PLANE * tok
+        and reach < LOOKBACK_WINDOW
+        and 2 * keys.shape[1] // n_heads >= tok
+        and (out_weight.shape[1] // n_ctx) % 128 == 0
+        and keys.shape[1] // n_heads % HEAD_SIZE == 0
+    )
 
 
 def passed_along(block, axis, distance):
@@ -97,4 +621,14 @@
         P("heads", "ctx"),
     )
     out_specs = P("ctx", "heads")
-    return jax.shard_map(body, mesh=mesh, in_specs=in_specs, out_specs=out_specs, check_vma=False)
+
+    def run(queries, keys, values, doc_ids, out_weight):
+        n_ctx, n_heads = mesh.shape["ctx"], mesh.shape["heads"]
+        local = body
+        if fits_fused(n_ctx, n_heads, queries, keys, out_weight):
+            local = functools.partial(fused_body, n_ctx, n_heads)
+        return jax.shard_map(
+            local, mesh=mesh, in_specs=in_specs, out_specs=out_specs, check_vma=False
+        )(queries, keys, values, doc_ids, out_weight)
+
+    return run

time: 400 us -> 164 us (0.41)
  waiting for transfers between devices: 172 us -> 0 us
  Pallas kernels: 0 us -> 158 us
  starting transfers between devices: 93.6 us -> 0 us
  matrix products: 63 us -> 0 us
  local copies, waits for them, and re-layouts: 31.1 us -> 2.32 us
  other arithmetic: 21.2 us -> 2.57 us
  between operations: 13.5 us -> 0.01 us
    pallas_call x0 -> x1, Pallas kernels: none -> 158 us  [fused_body(): pl.pallas_call(functools.partial(fused_kernel, planes, n_heads, groups, t...]
    ppermute x48 -> x0, waiting for transfers between devices: 139 us -> none  [passed_along(): return lax.ppermute(block, axis, route)]
    ppermute x48 -> x0, starting transfers between devices: 93.6 us -> none  [passed_along(): return lax.ppermute(block, axis, route)]
    dot_general x35 -> x0, matrix products: 63 us -> none  [the longest x17 36.5 us: work(): jnp.einsum('tgns,sgh->tgnh', rounded, vblk.reshape(tok_rows, groups, HEAD...]
    reduce_scatter x1 -> x0, waiting for transfers between devices: 32 us -> none  [body(): lax.psum_scatter(partial_sums.astype(jnp.bfloat16), 'heads', scatter_dime...]
    while x129 -> x0, local copies, waits for them, and re-layouts: 22.8 us -> none
    reduce_sum x17 -> x0, other arithmetic: 17.6 us -> none  [work(): total = total * factor + jnp.sum(weights, axis=-1)]
  transfers between devices with their start and end apart: 50 -> 0, of which waited for: 35 -> 0; matrix products, arithmetic and copies ran while one was open for 21% -> 0% of each run, Pallas kernels for 0% -> 0%
where the time goes in v1:
time: 164 us; the launch traced here: 163 us
  Pallas kernels  158 us (96%)
  other arithmetic  2.57 us (2%)
  local copies, waits for them, and re-layouts  2.32 us (1%)
    pallas_call x1, Pallas kernels, fused_body(): pl.pallas_call(functools.partial(fused_kernel, planes, n_heads, groups, t...  158 us

profile of v1, /device:TPU:24, one launch (start us, length us, event | category | flops | bytes accessed | tf_op | source)
XLA Modules:
  0.0 162.6 jit_solution(8286297918478219154)
XLA Ops:
  0.0 0.7 convert_element_type.5
  0.7 1.9 %pad_maximum_fusion.kv_hbm = bf16[272,1024]{1,0:T(8,128)(2,1)} fusion(bf16[16,1024]{1,0:T(8,128)(2,1)S(1)} %broadcast_in_dim.2, bf16[256,512]{1,0:T(8,128)(2,1)} %param.7, bf16[256,512]{1,0:T(8,128)(2,1)} %param.6), kind=kLoop, calls=%fused_computation | loop fusion | flops 1671168 | bytes 1114112 | tf_op jit(solution)/shard_map/concatenate | solution.py:471
  2.6 157.7 %shard_map.55 = bf16[256,2048]{1,0:T(8,128)(2,1)} custom-call(bf16[256,2048]{1,0:T(8,128)(2,1)} %q_ref.1, bf16[272,1024]{1,0:T(8,128)(2,1)} %pad_maximum_fusion.kv_hbm, bf16[2048,256]{1,0:T(8,128)(2,1)} %w_hbm.1), custom_call_target="tpu_custom_call" | custom-call | tf_op jit(solution)/shard_map/pallas_call | solution.py:474
  160.3 2.3 %copy.7 = bf16[256,2048]{1,0:T(8,128)(2,1)} copy(bf16[256,2048]{1,0:T(8,128)(2,1)} %shard_map.55) | data formatting | bytes 2097152
  (2 shorter events, 0.0 us)

commit v2 on v1

--- a/solution.py
+++ b/solution.py
@@ -39,6 +39,7 @@
     kdim = groups * HEAD_SIZE
     span = QPG * groups
     per_half = planes // n_heads
+    half = wcols // 2
 
     def in_plane(other):
         return (h, z * PLANE + other)
@@ -70,14 +71,36 @@
             kvbuf.at[d, who], kvbuf.at[d, who], kvf_send.at[d], kv_recv.at[d, who], in_plane(mate)
         ).wait_recv()
 
-    def w_up(j):
-        return copy(wbuf.at[j], wbuf.at[j], w_right.at[j], w_recv.at[j], up)
-
-    def w_down(j):
-        return copy(wbuf.at[j], wbuf.at[j], w_left.at[j], w_recv.at[j], down)
-
-    def w_wait(j):
-        copy(wbuf.at[j], wbuf.at[j], w_left.at[j], w_recv.at[j], in_plane(mate)).wait_recv()
+    def w_up(j, s):
+        ref = wbuf.at[j, s]
+        return copy(ref, ref, w_right.at[j, s], w_recv.at[j, s], up)
+
+    def w_down(j, s):
+        ref = wbuf.at[j, s]
+        return copy(ref, ref, w_left.at[j, s], w_recv.at[j, s], down)
+
+    def w_wait(j, s):
+        ref = wbuf.at[j, s]
+        copy(ref, ref, w_left.at[j, s], w_recv.at[j, s], in_plane(mate)).wait_recv()
+
+    def w_from_above(j):
+        for s in range(2):
+            w_wait(j, s)
+
+            @pl.when(z > 0)
+            def _():
+                w_down(j, s).start()
+
+    def w_from_below(j):
+        for s in range(2):
+            w_wait(j, s)
+
+            @pl.when(z < last)
+            def _():
+                w_up(j, s).start()
+
+    def target(k):
+        return jnp.where(k == 0, across, jnp.where(k == 1, diag, jnp.where(k == 2, mate, p)))
 
     def a_side(which):
         dev = in_plane(mate if which == 0 else across)
@@ -89,20 +112,26 @@
     def a_wait(who):
         copy(abuf.at[who], abuf.at[who], a_fwd, a_recv.at[who], in_plane(mate)).wait_recv()
 
-    def x_copy(jj, pp):
+    def x_copy(u, pp):
         return copy(
-            xsend.at[jj, pp], xrecv.at[jj, pp], x_send.at[jj, pp], x_recv.at[jj, pp], (1 - h, c)
-        )
-
-    def o_copy(jj, pp):
+            xsend.at[u, pp], xrecv.at[u, pp], x_send.at[u, pp], x_recv.at[u, pp], (1 - h, c)
+        )
+
+    def o_copy(u, pp):
         return copy(
-            rsend.at[jj, pp], obuf.at[jj, p], o_send.at[jj, pp], o_recv.at[jj, p], in_plane(pp)
+            rsend.at[u, pp], obuf.at[u, p], o_send.at[u, pp], o_recv.at[u, p], in_plane(pp)
         )
 
     kv_in = pltpu.make_async_copy(kv_hbm, kvbuf.at[0, p], local_sem.at[0])
-    w_in = pltpu.make_async_copy(w_hbm, wbuf.at[z], local_sem.at[1])
+    w_in = [
+        pltpu.make_async_copy(
+            w_hbm.at[:, s * half : (s + 1) * half], wbuf.at[z, s], local_sem.at[1 + s]
+        )
+        for s in range(2)
+    ]
     kv_in.start()
-    w_in.start()
+    w_in[0].start()
+    w_in[1].start()
 
     barrier = pltpu.get_barrier_semaphore()
     for dev in (in_plane(mate), in_plane(across), in_plane(diag), (1 - h, c)):
@@ -132,11 +161,13 @@
     def _():
         kv_side(0, 0).start()
 
-    w_in.wait()
+    w_in[0].wait()
+    w_in[1].wait()
 
     @pl.when(z > 0)
     def _():
-        w_down(z).start()
+        w_down(z, 0).start()
+        w_down(z, 1).start()
 
     factor = HEAD_SIZE ** (-0.5) * math.log2(math.e)
 
@@ -199,7 +230,8 @@
 
     @pl.when(z < last)
     def _():
-        w_up(z).start()
+        w_up(z, 0).start()
+        w_up(z, 1).start()
 
     @pl.when(row == 1)
     def _():
@@ -242,17 +274,21 @@
 
     @pl.when(z < last)
     def _():
-        w_wait(z + 1)
-
-        @pl.when(z > 0)
-        def _():
-            w_down(z + 1).start()
+        w_from_above(z + 1)
 
     @pl.when(z > 0)
     def _():
         kv_wait(1, mate)
         kv_wait(1, diag)
         block_loop(1, 0, PLANE)
+
+    @pl.when(z > 0)
+    def _():
+        w_from_below(z - 1)
+
+    @pl.when(z + 2 < planes)
+    def _():
+        w_from_above(z + 2)
 
     @pl.when(z > 1)
     def _():
@@ -280,21 +316,9 @@
     a_side(1).start()
     a_side(0).start()
 
-    @pl.when(z > 0)
-    def _():
-        w_wait(z - 1)
-
-        @pl.when(z < last)
-        def _():
-            w_up(z - 1).start()
-
-    @pl.when(z + 2 < planes)
-    def _():
-        w_wait(z + 2)
-
-        @pl.when(z > 0)
-        def _():
-            w_down(z + 2).start()
+    @pl.when(z > 1)
+    def _():
+        w_from_below(z - 2)
 
     a_wait(across)
     a_forward().start()
@@ -305,98 +329,123 @@
         dist = (i + 1) // 2
         return z + dist * (2 * (i % 2) - 1)
 
+    def exists(j):
+        return (j >= 0) & (j < planes)
+
+    def place(u, pp, part):
+        j = u // 2
+        mine = (j // per_half) == h
+        uu = u % (2 * per_half)
+
+        @pl.when(mine)
+        def _():
+            keep[uu, pp] = part
+
+        @pl.when(jnp.logical_not(mine))
+        def _():
+            xsend[uu, pp] = part.astype(jnp.bfloat16)
+            x_copy(uu, pp).start()
+
     def project(i):
         j = plane_of(i)
 
-        @pl.when((j >= 0) & (j < planes))
-        def _():
-            @pl.when(i >= 4)
+        @pl.when(exists(j))
+        def _():
+            @pl.when(i >= 5)
             def _():
-                w_wait(j)
-
-                @pl.when((j < z) & (z < last))
-                def _():
-                    w_up(j).start()
-
-                @pl.when((j > z) & (z > 0))
-                def _():
-                    w_down(j).start()
-
-            jj = j % per_half
-            mine = (j // per_half) == h
+                w_wait(j, 0)
+                w_wait(j, 1)
 
             def rows(k, carry):
-                pp = (p + 1 + k) % PLANE
-                part = jnp.dot(abuf[pp], wbuf[j], preferred_element_type=jnp.float32)
-
-                @pl.when(mine)
-                def _():
-                    keep[jj, pp] = part
-
-                @pl.when(jnp.logical_not(mine))
-                def _():
-                    xsend[jj, pp] = part.astype(jnp.bfloat16)
-                    x_copy(jj, pp).start()
-
+                pp = target(k)
+                both = jnp.concatenate([wbuf[j, 0], wbuf[j, 1]], axis=1)
+                part = jnp.dot(abuf[pp], both, preferred_element_type=jnp.float32)
+                place(2 * j, pp, part[:, :half])
+                place(2 * j + 1, pp, part[:, half:])
                 return carry
 
             lax.fori_loop(0, PLANE, rows, 0)
 
-    def finish(i):
+    def project_half(i, s):
         j = plane_of(i)
 
-        @pl.when((j >= 0) & (j < planes) & ((j // per_half) == h))
-        def _():
-            jj = j % per_half
+        @pl.when(exists(j))
+        def _():
+            w_wait(j, s)
 
             def rows(k, carry):
-                pp = (p + 1 + k) % PLANE
-                x_copy(jj, pp).wait_recv()
-                done = (keep[jj, pp] + xrecv[jj, pp].astype(jnp.float32)).astype(jnp.bfloat16)
+                pp = target(k)
+                part = jnp.dot(abuf[pp], wbuf[j, s], preferred_element_type=jnp.float32)
+                place(2 * j + s, pp, part)
+                return carry
+
+            lax.fori_loop(0, PLANE, rows, 0)
+
+    def finish(i, s):
+        j = plane_of(i)
+
+        @pl.when(exists(j) & ((j // per_half) == h))
+        def _():
+            u = (2 * j + s) % (2 * per_half)
+
+            def rows(k, carry):
+                pp = target(k)
+                x_copy(u, pp).wait_recv()
+                done = (keep[u, pp] + xrecv[u, pp].astype(jnp.float32)).astype(jnp.bfloat16)
 
                 @pl.when(pp == p)
                 def _():
-                    at = pl.multiple_of((jj * PLANE + p) * wcols, wcols)
-                    out_ref[:, pl.ds(at, wcols)] = done
+                    out_ref[:, column(u, p)] = done
 
                 @pl.when(pp != p)
                 def _():
-                    rsend[jj, pp] = done
-                    o_copy(jj, pp).start()
+                    rsend[u, pp] = done
+                    o_copy(u, pp).start()
 
                 return carry
 
             lax.fori_loop(0, PLANE, rows, 0)
 
+    def column(u, src):
+        return pl.ds(pl.multiple_of(((u // 2) * PLANE + src) * wcols + (u % 2) * half, half), half)
+
     steps = 2 * planes - 1
-    project(0)
-
-    def step(i, carry):
+
+    def project_step(i, carry):
         project(i)
-        finish(i - 1)
         return carry
 
-    lax.fori_loop(1, steps, step, 0)
-    finish(steps - 1)
+    def finish_step(k, carry):
+        finish(k // 2, k % 2)
+        return carry
+
+    lax.fori_loop(0, steps - 1, project_step, 0)
+    lax.fori_loop(0, 2 * (steps - 1), finish_step, 0)
+
+    def far_project(s, carry):
+        project_half(steps - 1, s)
+        return carry
+
+    lax.fori_loop(0, 2, far_project, 0)
+    lax.fori_loop(2 * (steps - 1), 2 * steps, finish_step, 0)
 
     def collect(k, carry):
-        jj = k // PLANE
+        u = k // PLANE
         src = k % PLANE
 
         @pl.when(src != p)
         def _():
             copy(
-                obuf.at[jj, src], obuf.at[jj, src], o_send.at[jj, src], o_recv.at[jj, src],
+                obuf.at[u, src], obuf.at[u, src], o_send.at[u, src], o_recv.at[u, src],
                 in_plane(mate),
             ).wait_recv()
-            at = pl.multiple_of(k * wcols, wcols)
-            out_ref[:, pl.ds(at, wcols)] = obuf[jj, src]
-            o_copy(jj, src).wait_send()
-
-        x_copy(jj, src).wait_send()
+            out_ref[:, column(u, src)] = obuf[u, src]
+            o_copy(u, src).wait_send()
+
+        x_copy(u, src).wait_send()
         return carry
 
-    lax.fori_loop(0, per_half * PLANE, collect, 0)
+    lax.fori_loop(0, 2 * per_half * PLANE, collect, 0)
 
     a_side(0).wait_send()
     a_side(1).wait_send()
@@ -405,11 +454,13 @@
     def w_drain(j, carry):
         @pl.when((j <= z) & (z < last))
         def _():
-            w_up(j).wait_send()
+            w_up(j, 0).wait_send()
+            w_up(j, 1).wait_send()
 
         @pl.when((j >= z) & (z > 0))
         def _():
-            w_down(j).wait_send()
+            w_down(j, 0).wait_send()
+            w_down(j, 1).wait_send()
 
         return carry
 
@@ -482,32 +533,32 @@
         out_specs=pl.BlockSpec(memory_space=pltpu.VMEM),
         scratch_shapes=[
             pltpu.VMEM((3, PLANE, tok + DOC_ROWS, width), bf),
-            pltpu.VMEM((planes, krows, wcols), bf),
+            pltpu.VMEM((planes, 2, krows, wcols // 2), bf),
             pltpu.VMEM((PLANE, tok, krows), bf),
             pltpu.VMEM((span, HEAD_SIZE, tok), f32),
             pltpu.VMEM((span, 1, tok), f32),
             pltpu.VMEM((span, 1, tok), f32),
             pltpu.VMEM((tok, tok), f32),
-            pltpu.VMEM((per_half, PLANE, tok, wcols), bf),
-            pltpu.VMEM((per_half, PLANE, tok, wcols), bf),
-            pltpu.VMEM((per_half, PLANE, tok, wcols), f32),
-            pltpu.VMEM((per_half, PLANE, tok, wcols), bf),
-            pltpu.VMEM((per_half, PLANE, tok, wcols), bf),
-            dma((2,)),
+            pltpu.VMEM((2 * per_half, PLANE, tok, wcols // 2), bf),
+            pltpu.VMEM((2 * per_half, PLANE, tok, wcols // 2), bf),
+            pltpu.VMEM((2 * per_half, PLANE, tok, wcols // 2), f32),
+            pltpu.VMEM((2 * per_half, PLANE, tok, wcols // 2), bf),
+            pltpu.VMEM((2 * per_half, PLANE, tok, wcols // 2), bf),
+            dma((3,)),
             dma((3, PLANE)),
             dma((2,)),
             dma((3, 2)),
             dma((3,)),
-            dma((planes,)),
-            dma((planes,)),
-            dma((planes,)),
+            dma((planes, 2)),
+            dma((planes, 2)),
+            dma((planes, 2)),
             dma((PLANE,)),
             dma((2,)),
             dma,
-            dma((per_half, PLANE)),
-            dma((per_half, PLANE)),
-            dma((per_half, PLANE)),
-            dma((per_half, PLANE)),
+            dma((2 * per_half, PLANE)),
+            dma((2 * per_half, PLANE)),
+            dma((2 * per_half, PLANE)),
+            dma((2 * per_half, PLANE)),
         ],
         compiler_params=pltpu.CompilerParams(
             collective_id=0, has_side_effects=True, vmem_limit_bytes=56 * 1024 * 1024
@@ -527,7 +578,7 @@
         and reach == 2 * PLANE * tok
         and reach < LOOKBACK_WINDOW
         and 2 * keys.shape[1] // n_heads >= tok
-        and (out_weight.shape[1] // n_ctx) % 128 == 0
+        and (out_weight.shape[1] // n_ctx) % 256 == 0
         and keys.shape[1] // n_heads % HEAD_SIZE == 0
     )
 

time: 164 us -> 141 us (0.86)
  Pallas kernels: 158 us -> 136 us
    pallas_call x1, Pallas kernels: 158 us -> 136 us  [fused_body(): pl.pallas_call(functools.partial(fused_kernel, planes, n_heads, groups, t...]
where the time goes in v2:
time: 141 us
  Pallas kernels  136 us (96%)
  other arithmetic  2.57 us (2%)
  local copies, waits for them, and re-layouts  2.32 us (2%)
    pallas_call x1, Pallas kernels, fused_body(): pl.pallas_call(functools.partial(fused_kernel, planes, n_heads, groups, t...  136 us

profile of v2, /device:TPU:24, one launch (start us, length us, event | category | flops | bytes accessed | tf_op | source)
XLA Modules:
  0.0 141.3 jit_solution(10499098949132119768)
XLA Ops:
  0.0 0.7 convert_element_type.5
  0.7 1.9 %pad_maximum_fusion.kv_hbm = bf16[272,1024]{1,0:T(8,128)(2,1)} fusion(bf16[16,1024]{1,0:T(8,128)(2,1)S(1)} %broadcast_in_dim.2, bf16[256,512]{1,0:T(8,128)(2,1)} %param.7, bf16[256,512]{1,0:T(8,128)(2,1)} %param.6), kind=kLoop, calls=%fused_computation | loop fusion | flops 1671168 | bytes 1114112 | tf_op jit(solution)/shard_map/concatenate | solution.py:522
  2.6 136.4 %shard_map.55 = bf16[256,2048]{1,0:T(8,128)(2,1)} custom-call(bf16[256,2048]{1,0:T(8,128)(2,1)} %q_ref.1, bf16[272,1024]{1,0:T(8,128)(2,1)} %pad_maximum_fusion.kv_hbm, bf16[2048,256]{1,0:T(8,128)(2,1)} %w_hbm.1), custom_call_target="tpu_custom_call" | custom-call | tf_op jit(solution)/shard_map/pallas_call | solution.py:525
  139.0 2.3 %copy.7 = bf16[256,2048]{1,0:T(8,128)(2,1)} copy(bf16[256,2048]{1,0:T(8,128)(2,1)} %shard_map.55) | data formatting | bytes 2097152
  (2 shorter events, 0.0 us)

commit v3 on v2

--- a/solution.py
+++ b/solution.py
@@ -420,14 +420,12 @@
         return carry
 
     lax.fori_loop(0, steps - 1, project_step, 0)
-    lax.fori_loop(0, 2 * (steps - 1), finish_step, 0)
-
     def far_project(s, carry):
         project_half(steps - 1, s)
         return carry
 
     lax.fori_loop(0, 2, far_project, 0)
-    lax.fori_loop(2 * (steps - 1), 2 * steps, finish_step, 0)
+    lax.fori_loop(0, 2 * steps, finish_step, 0)
 
     def collect(k, carry):
         u = k // PLANE

time: 141 us -> 135 us (0.957); the launches traced: 141 us -> 133 us
  Pallas kernels: 136 us -> 128 us
    pallas_call x1, Pallas kernels: 136 us -> 128 us  [fused_body(): pl.pallas_call(functools.partial(fused_kernel, planes, n_heads, groups, t...]
where the time goes in v3:
time: 135 us; the launch traced here: 133 us
  Pallas kernels  128 us (95%)
  other arithmetic  2.57 us (2%)
  local copies, waits for them, and re-layouts  2.32 us (2%)
    pallas_call x1, Pallas kernels, fused_body(): pl.pallas_call(functools.partial(fused_kernel, planes, n_heads, groups, t...  128 us

profile of v3, /device:TPU:24, one launch (start us, length us, event | category | flops | bytes accessed | tf_op | source)
XLA Modules:
  0.0 133.4 jit_solution(11901493470367291659)
XLA Ops:
  0.0 0.7 convert_element_type.5
  0.7 1.9 %pad_maximum_fusion.kv_hbm = bf16[272,1024]{1,0:T(8,128)(2,1)} fusion(bf16[16,1024]{1,0:T(8,128)(2,1)S(1)} %broadcast_in_dim.2, bf16[256,512]{1,0:T(8,128)(2,1)} %param.7, bf16[256,512]{1,0:T(8,128)(2,1)} %param.6), kind=kLoop, calls=%fused_computation | loop fusion | flops 1671168 | bytes 1114112 | tf_op jit(solution)/shard_map/concatenate | solution.py:520
  2.6 128.4 %shard_map.55 = bf16[256,2048]{1,0:T(8,128)(2,1)} custom-call(bf16[256,2048]{1,0:T(8,128)(2,1)} %q_ref.1, bf16[272,1024]{1,0:T(8,128)(2,1)} %pad_maximum_fusion.kv_hbm, bf16[2048,256]{1,0:T(8,128)(2,1)} %w_hbm.1), custom_call_target="tpu_custom_call" | custom-call | tf_op jit(solution)/shard_map/pallas_call | solution.py:523
  131.0 2.3 %copy.7 = bf16[256,2048]{1,0:T(8,128)(2,1)} copy(bf16[256,2048]{1,0:T(8,128)(2,1)} %shard_map.55) | data formatting | bytes 2097152
  (2 shorter events, 0.0 us)

commit v4 on v3

--- a/solution.py
+++ b/solution.py
@@ -282,11 +282,11 @@
         kv_wait(1, diag)
         block_loop(1, 0, PLANE)
 
-    @pl.when(z > 0)
+    @pl.when((z > 0) & (z < last))
     def _():
         w_from_below(z - 1)
 
-    @pl.when(z + 2 < planes)
+    @pl.when((z > 0) & (z + 2 < planes))
     def _():
         w_from_above(z + 2)
 
@@ -316,14 +316,17 @@
     a_side(1).start()
     a_side(0).start()
 
+    @pl.when(z == last)
+    def _():
+        w_from_below(z - 1)
+
+    @pl.when((z == 0) & (z + 2 < planes))
+    def _():
+        w_from_above(z + 2)
+
     @pl.when(z > 1)
     def _():
         w_from_below(z - 2)
-
-    a_wait(across)
-    a_forward().start()
-    a_wait(mate)
-    a_wait(diag)
 
     def plane_of(i):
         dist = (i + 1) // 2
@@ -346,7 +349,7 @@
             xsend[uu, pp] = part.astype(jnp.bfloat16)
             x_copy(uu, pp).start()
 
-    def project(i):
+    def project(i, lo, hi):
         j = plane_of(i)
 
         @pl.when(exists(j))
@@ -364,7 +367,7 @@
                 place(2 * j + 1, pp, part[:, half:])
                 return carry
 
-            lax.fori_loop(0, PLANE, rows, 0)
+            lax.fori_loop(lo, hi, rows, 0)
 
     def project_half(i, s):
         j = plane_of(i)
@@ -411,15 +414,25 @@
 
     steps = 2 * planes - 1
 
-    def project_step(i, carry):
-        project(i)
+    def near_step(i, carry):
+        project(i, 2, PLANE)
+        return carry
+
+    def across_step(i, carry):
+        project(i, 0, 2)
         return carry
 
     def finish_step(k, carry):
         finish(k // 2, k % 2)
         return carry
 
-    lax.fori_loop(0, steps - 1, project_step, 0)
+    a_wait(mate)
+    lax.fori_loop(0, steps - 2, near_step, 0)
+    a_wait(across)
+    a_forward().start()
+    a_wait(diag)
+    lax.fori_loop(0, steps - 2, across_step, 0)
+    project(steps - 2, 0, PLANE)
     def far_project(s, carry):
         project_half(steps - 1, s)
         return carry

time: 135 us -> 126 us (0.933)
  Pallas kernels: 128 us -> 121 us
    pallas_call x1, Pallas kernels: 128 us -> 121 us  [fused_body(): pl.pallas_call(functools.partial(fused_kernel, planes, n_heads, groups, t...]
where the time goes in v4:
time: 126 us; the launch traced here: 125 us
  Pallas kernels  121 us (96%)
  other arithmetic  2.57 us (2%)
  local copies, waits for them, and re-layouts  2.32 us (2%)
    pallas_call x1, Pallas kernels, fused_body(): pl.pallas_call(functools.partial(fused_kernel, planes, n_heads, groups, t...  121 us

profile of v4, /device:TPU:24, one launch (start us, length us, event | category | flops | bytes accessed | tf_op | source)
XLA Modules:
  0.0 125.4 jit_solution(13938549331121659575)
XLA Ops:
  0.0 0.7 convert_element_type.5
  0.7 1.9 %pad_maximum_fusion.kv_hbm = bf16[272,1024]{1,0:T(8,128)(2,1)} fusion(bf16[16,1024]{1,0:T(8,128)(2,1)S(1)} %broadcast_in_dim.2, bf16[256,512]{1,0:T(8,128)(2,1)} %param.7, bf16[256,512]{1,0:T(8,128)(2,1)} %param.6), kind=kLoop, calls=%fused_computation | loop fusion | flops 1671168 | bytes 1114112 | tf_op jit(solution)/shard_map/concatenate | solution.py:533
  2.6 120.5 %shard_map.55 = bf16[256,2048]{1,0:T(8,128)(2,1)} custom-call(bf16[256,2048]{1,0:T(8,128)(2,1)} %q_ref.1, bf16[272,1024]{1,0:T(8,128)(2,1)} %pad_maximum_fusion.kv_hbm, bf16[2048,256]{1,0:T(8,128)(2,1)} %w_hbm.1), custom_call_target="tpu_custom_call" | custom-call | tf_op jit(solution)/shard_map/pallas_call | solution.py:536
  123.1 2.3 %copy.7 = bf16[256,2048]{1,0:T(8,128)(2,1)} copy(bf16[256,2048]{1,0:T(8,128)(2,1)} %shard_map.55) | data formatting | bytes 2097152
  (2 shorter events, 0.0 us)
